TPU v7x, 32 devices: a whole 2x2x4 slice. The times are simulated.
32 devices in a mesh: row: 4 (over y, x), col: 8 (over z, core).
Axes of the slice: x: 2, y: 2, z: 4, core: 2. Of those that a mesh axis runs over, the one named last changes fastest.
Arguments:
- incoming_optic_cosine_part: float32 [2048, 2048], P('row', 'col'), may hold values from -6 to 6
- incoming_optic_sine_part: float32 [2048, 2048], P('row', 'col'), may hold values from -6 to 6
- weak_pulse_growth_rate: float32 [2048, 2048], P('row', 'col'), may hold values from 0.5 to 2
- thermal_rise_beforehand: float32 [8, 2048, 2048], P('row', None, 'col'), may hold values from -6 to 6
- lengthwise_slice_pick: int32 [2], replicated, may hold values from 0 to 7
Outputs:
- temperature_out: float32 [8, 2048, 2048], P('row', None, 'col')
- beam_out_real: float32 [2048, 2048], P('row', 'col')
- beam_out_imag: float32 [2048, 2048], P('row', 'col')
Inputs may be any that keep to these rules, and one draw needn't show every extreme that they name: Step k deposits into plane lengthwise_slice_pick[k]; planes may repeat.
All inputs are finite; a program needn't handle non-finite values.
Results may differ from a plain program's by a relative error of at most 0.0001.
Values sent between devices are 32-bit elements; how exact they have to be, the bound alone decides.
A program may use at most 192 MiB of HBM per device.

v0:
```python
import math

import jax
import jax.numpy as jnp
from jax import lax
from jax.sharding import PartitionSpec as P

MESH_WIDTH = 2048
STEPS = 2
SWEEPS = 2


FLUENCE_LIMIT = 2.0
GAIN_LENGTH = 0.2
INDEX_SLOPE_DNDT = 0.3


def padded(cells, sides, width):
    for axis, dim in sides:
        count = lax.axis_size(axis)
        ends = count - 1
        head = lax.slice_in_dim(cells, 0, width, axis=dim)
        tail = lax.slice_in_dim(cells, cells.shape[dim] - width, cells.shape[dim], axis=dim)
        cells = jnp.concatenate(
            [
                lax.ppermute(tail, axis, [(i, (i + 1) % count) for i in range(ends)]),
                cells,
                lax.ppermute(head, axis, [((i + 1) % count, i) for i in range(ends)]),
            ],
            axis=dim,
        )
    return cells


def adjacent_cells(border_extended):
    total = border_extended[2:, 1:-1, 1:-1] + border_extended[:-2, 1:-1, 1:-1]
    total = total + border_extended[1:-1, 2:, 1:-1] + border_extended[1:-1, :-2, 1:-1]
    total = total + border_extended[1:-1, 1:-1, 2:] + border_extended[1:-1, 1:-1, :-2]
    return total


def chirp_index(index_values):
    return index_values * index_values % (2 * MESH_WIDTH)


def angle_table(outer_len, inner_len, modulus):
    first = lax.iota(jnp.int32, outer_len)
    second = lax.iota(jnp.int32, inner_len)
    return (first[:, None] * second[None, :] % modulus).astype(jnp.float32) * (
        2.0 * math.pi / modulus
    )


def transform_last(real_part, imag_part, sign):
    length = real_part.shape[-1]
    leading = real_part.shape[:-1]
    small = 2 ** ((length.bit_length() - 1) // 2)
    large = length // small
    first_angles = angle_table(large, large, large)
    first_cos = jnp.cos(first_angles)
    first_sin = sign * jnp.sin(first_angles)
    twiddle_angles = angle_table(large, small, length)
    twiddle_cos = jnp.cos(twiddle_angles)
    twiddle_sin = sign * jnp.sin(twiddle_angles)
    second_angles = angle_table(small, small, small)
    second_cos = jnp.cos(second_angles)
    second_sin = sign * jnp.sin(second_angles)
    highest = lax.Precision.HIGHEST
    real_blocks = real_part.reshape(leading + (large, small))
    imag_blocks = imag_part.reshape(leading + (large, small))

    def section_one(values, table):
        return jnp.einsum("...np,kn->...kp", values, table, precision=highest)

    real_mid = section_one(real_blocks, first_cos) - section_one(imag_blocks, first_sin)
    imag_mid = section_one(imag_blocks, first_cos) + section_one(real_blocks, first_sin)
    real_tw = real_mid * twiddle_cos - imag_mid * twiddle_sin
    imag_tw = imag_mid * twiddle_cos + real_mid * twiddle_sin

    def section_two(values, table):
        return jnp.einsum("...kp,jp->...kj", values, table, precision=highest)

    real_out = section_two(real_tw, second_cos) - section_two(imag_tw, second_sin)
    imag_out = section_two(imag_tw, second_cos) + section_two(real_tw, second_sin)
    real_out = jnp.swapaxes(real_out, -1, -2).reshape(leading + (length,))
    imag_out = jnp.swapaxes(imag_out, -1, -2).reshape(leading + (length,))
    return (real_out, imag_out)


def transform_first(real_part, imag_part, sign):
    real_out, imag_out = transform_last(real_part.T, imag_part.T, sign)
    return (real_out.T, imag_out.T)


def shards(
    incoming_optic_cosine_part,
    incoming_optic_sine_part,
    weak_pulse_growth_rate,
    thermal_rise_beforehand,
    lengthwise_slice_pick,
):
    positions = lax.iota(jnp.int32, MESH_WIDTH)
    row_index = lax.axis_index("row")
    col_index = lax.axis_index("col")
    col_count = lax.axis_size("col")
    real_part = incoming_optic_cosine_part
    imag_part = incoming_optic_sine_part
    strip_list = []
    axial_layer_array = thermal_rise_beforehand.shape[0]
    tile_cols = thermal_rise_beforehand.shape[2]
    plane_ids = row_index * axial_layer_array + lax.iota(jnp.int32, axial_layer_array)
    deposited_power = jnp.zeros(thermal_rise_beforehand.shape, jnp.float32)
    for step in range(STEPS):
        real_part, imag_part = (
            lax.all_to_all(real_part, "col", split_axis=0, concat_axis=1, tiled=True),
            lax.all_to_all(imag_part, "col", split_axis=0, concat_axis=1, tiled=True),
        )
        real_part, imag_part = transform_last(real_part, imag_part, -1.0)
        real_part, imag_part = (
            lax.all_to_all(real_part, ("row", "col"), split_axis=1, concat_axis=0, tiled=True),
            lax.all_to_all(imag_part, ("row", "col"), split_axis=1, concat_axis=0, tiled=True),
        )
        real_part, imag_part = transform_first(real_part, imag_part, -1.0)
        width = real_part.shape[1]
        first_col = (row_index * col_count + col_index) * width
        row_chirp = chirp_index(positions)
        col_chirp = chirp_index(first_col + lax.iota(jnp.int32, width))
        phase_index = (row_chirp[:, None] + col_chirp[None, :]) % (2 * MESH_WIDTH)
        phase = math.pi * phase_index.astype(jnp.float32) / MESH_WIDTH
        kernel_cos = jnp.cos(phase)
        kernel_sin = jnp.sin(phase)
        real_part, imag_part = (
            real_part * kernel_cos + imag_part * kernel_sin,
            imag_part * kernel_cos - real_part * kernel_sin,
        )
        real_part, imag_part = transform_first(real_part, imag_part, 1.0)
        real_part = real_part / MESH_WIDTH
        imag_part = imag_part / MESH_WIDTH
        real_part, imag_part = (
            lax.all_to_all(real_part, ("row", "col"), split_axis=0, concat_axis=1, tiled=True),
            lax.all_to_all(imag_part, ("row", "col"), split_axis=0, concat_axis=1, tiled=True),
        )
        real_part, imag_part = transform_last(real_part, imag_part, 1.0)
        real_part = real_part / MESH_WIDTH
        imag_part = imag_part / MESH_WIDTH
        real_part, imag_part = (
            lax.all_to_all(real_part, "col", split_axis=1, concat_axis=0, tiled=True),
            lax.all_to_all(imag_part, "col", split_axis=1, concat_axis=0, tiled=True),
        )
        irradiance = real_part**2 + imag_part**2
        bleaching_factor = weak_pulse_growth_rate / (1.0 + irradiance / FLUENCE_LIMIT)
        heat = bleaching_factor * irradiance
        amplify = jnp.exp(0.5 * GAIN_LENGTH * bleaching_factor)
        real_part = real_part * amplify
        imag_part = imag_part * amplify
        strip = lax.all_gather(heat, "row", axis=0, tiled=True)
        strip_list.append(strip)
        select = (plane_ids == lengthwise_slice_pick[step]).astype(jnp.float32)
        deposited_power = deposited_power + select[:, None, None] * strip[None]
    deep_temp = padded(thermal_rise_beforehand, (("row", 0), ("col", 2)), SWEEPS)
    rimmed = padded(jnp.stack(strip_list), (("col", 2),), SWEEPS)
    wide_ids = (
        row_index * axial_layer_array - SWEEPS + lax.iota(jnp.int32, axial_layer_array + 2 * SWEEPS)
    )
    deep_source = jnp.zeros(deep_temp.shape, jnp.float32)
    for step in range(STEPS):
        select = (wide_ids == lengthwise_slice_pick[step]).astype(jnp.float32)
        deep_source = deep_source + select[:, None, None] * rimmed[step][None]
    deep_rhs = deep_temp + deep_source
    margin_pad = ((0, 0), (SWEEPS, SWEEPS), (0, 0))
    present_warmth = jnp.pad(deep_temp, margin_pad)
    deep_rhs = jnp.pad(deep_rhs, margin_pad)
    total_planes = axial_layer_array * lax.axis_size("row")
    for sweep in range(SWEEPS):
        crop = sweep + 1
        edge = SWEEPS - crop
        rhs_inner = deep_rhs[
            crop : deep_rhs.shape[0] - crop,
            crop : deep_rhs.shape[1] - crop,
            crop : deep_rhs.shape[2] - crop,
        ]
        present_warmth = (rhs_inner + adjacent_cells(present_warmth)) / 7.0
        zpos = (
            row_index * axial_layer_array - edge + lax.iota(jnp.int32, axial_layer_array + 2 * edge)
        )
        xpos = lax.iota(jnp.int32, MESH_WIDTH + 2 * edge) - edge
        ypos = col_index * tile_cols - edge + lax.iota(jnp.int32, tile_cols + 2 * edge)
        zmask = ((zpos >= 0) & (zpos < total_planes)).astype(jnp.float32)
        xmask = ((xpos >= 0) & (xpos < MESH_WIDTH)).astype(jnp.float32)
        ymask = ((ypos >= 0) & (ypos < tile_cols * col_count)).astype(jnp.float32)
        present_warmth = (
            present_warmth * zmask[:, None, None] * xmask[None, :, None] * ymask[None, None, :]
        )
    running_total = jnp.sum(present_warmth, axis=0)
    phase_angle = INDEX_SLOPE_DNDT * lax.psum_scatter(
        running_total, "row", scatter_dimension=0, tiled=True
    )
    leaving_inphase = real_part * jnp.cos(phase_angle) - imag_part * jnp.sin(phase_angle)
    leaving_quadrature = real_part * jnp.sin(phase_angle) + imag_part * jnp.cos(phase_angle)
    return (present_warmth, leaving_inphase, leaving_quadrature)


def solution(mesh):
    placed = (P("row", "col"), P("row", "col"), P("row", "col"), P("row", None, "col"), P())
    return jax.shard_map(
        shards,
        mesh=mesh,
        in_specs=placed,
        out_specs=(P("row", None, "col"), P("row", "col"), P("row", "col")),
        check_vma=False,
    )
```

profile of v0, /device:TPU:0, one launch (start us, length us, event | category | flops | bytes accessed | tf_op | source)
XLA Modules:
  0.0 912.3 jit_solution(14261556633360696807)
XLA Ops:
  7.2 21.7 %all_to_all.256 = f32[8,64,256]{2,1,0:T(8,128)S(1)} all-to-all(f32[8,64,256]{2,1,0:T(8,128)} %bitcast.449), channel_id=1, replica_groups=mesh['row'=4,'col'=8] {'col'}, dimensions={0} | all-to-all | bytes 1048576 | tf_op jit(solution)/shard_map/all_to_all | solution.py:116
  37.2 11.1 %all-to-all-done = f32[8,64,256]{2,1,0:T(8,128)} async-done(((f32[8,64,256]{2,1,0:T(8,128)}), f32[8,64,256]{2,1,0:T(8,128)}, u32[]{:S(2)}, u32[]{:S(2)}) %all-to-all-start) | async-done | bytes 524320 | tf_op jit(solution)/shard_map/all_to_all | solution.py:115
  66.1 14.3 %fusion.36 = f32[64,32,64]{2,1,0:T(8,128)S(1)} fusion(f32[64,64,32]{1,2,0:T(8,128)} %fusion.163, f32[64,64,32]{1,2,0:T(8,128)S(1)} %copy.446), kind=kOutput, calls=%fused_computation.88 | convolution fusion | flops 50478080 | bytes 1572864 | tf_op jit(solution)/shard_map/...kp,jp->...kj/dot_general | solution.py:81
  90.3 12.0 %all-to-all-done.2 = f32[32,1,4096]{2,1,0:T(1,128)S(1)} async-done(((f32[32,1,4096]{2,1,0:T(1,128)}), f32[32,1,4096]{2,1,0:T(1,128)S(1)}, u32[]{:S(2)}, u32[]{:S(2)}) %all-to-all-start.2) | async-done | bytes 524320 | tf_op jit(solution)/shard_map/all_to_all | solution.py:120
  108.6 12.5 %all-to-all-done.3 = f32[32,1,4096]{2,1,0:T(1,128)S(1)} async-done(((f32[32,1,4096]{2,1,0:T(1,128)}), f32[32,1,4096]{2,1,0:T(1,128)S(1)}, u32[]{:S(2)}, u32[]{:S(2)}) %all-to-all-start.3) | async-done | bytes 524320 | tf_op jit(solution)/shard_map/all_to_all | solution.py:121
  200.6 11.2 %all-to-all-done.4 = f32[32,1,4096]{2,1,0:T(1,128)S(1)} async-done(((f32[32,1,4096]{2,1,0:T(1,128)}), f32[32,1,4096]{2,1,0:T(1,128)S(1)}, u32[]{:S(2)}, u32[]{:S(2)}) %all-to-all-start.4) | async-done | bytes 524320 | tf_op jit(solution)/shard_map/all_to_all | solution.py:140
  217.4 13.3 %all-to-all-done.5 = f32[32,1,4096]{2,1,0:T(1,128)S(1)} async-done(((f32[32,1,4096]{2,1,0:T(1,128)}), f32[32,1,4096]{2,1,0:T(1,128)S(1)}, u32[]{:S(2)}, u32[]{:S(2)}) %all-to-all-start.5) | async-done | bytes 524320 | tf_op jit(solution)/shard_map/all_to_all | solution.py:141
  267.7 11.8 %all-to-all-done.6 = f32[64,8,256]{2,0,1:T(8,128)S(1)} async-done(((f32[64,8,256]{2,0,1:T(8,128)}), f32[64,8,256]{2,0,1:T(8,128)S(1)}, u32[]{:S(2)}, u32[]{:S(2)}) %all-to-all-start.6) | async-done | bytes 524320 | tf_op jit(solution)/shard_map/all_to_all | solution.py:147
  284.4 13.8 %all-to-all-done.7 = f32[64,8,256]{2,0,1:T(8,128)S(1)} async-done(((f32[64,8,256]{2,0,1:T(8,128)}), f32[64,8,256]{2,0,1:T(8,128)S(1)}, u32[]{:S(2)}, u32[]{:S(2)}) %all-to-all-start.7) | async-done | bytes 524320 | tf_op jit(solution)/shard_map/all_to_all | solution.py:148
  305.0 14.3 %all-to-all-done.9 = f32[8,64,256]{2,1,0:T(8,128)S(1)} async-done(((f32[8,64,256]{2,1,0:T(8,128)}), f32[8,64,256]{2,1,0:T(8,128)S(1)}, u32[]{:S(2)}, u32[]{:S(2)}) %all-to-all-start.9) | async-done | bytes 524320 | tf_op jit(solution)/shard_map/all_to_all | solution.py:116
  328.1 10.1 %all-to-all-done.8 = f32[8,64,256]{2,1,0:T(8,128)S(1)} async-done(((f32[8,64,256]{2,1,0:T(8,128)}), f32[8,64,256]{2,1,0:T(8,128)S(1)}, u32[]{:S(2)}, u32[]{:S(2)}) %all-to-all-start.8) | async-done | bytes 524320 | tf_op jit(solution)/shard_map/all_to_all | solution.py:115
  374.7 12.0 %all-to-all-done.10 = f32[32,1,4096]{2,1,0:T(1,128)S(1)} async-done(((f32[32,1,4096]{2,1,0:T(1,128)}), f32[32,1,4096]{2,1,0:T(1,128)S(1)}, u32[]{:S(2)}, u32[]{:S(2)}) %all-to-all-start.10) | async-done | bytes 524320 | tf_op jit(solution)/shard_map/all_to_all | solution.py:120
  393.2 13.2 %all-to-all-done.11 = f32[32,1,4096]{2,1,0:T(1,128)} async-done(((f32[32,1,4096]{2,1,0:T(1,128)}), f32[32,1,4096]{2,1,0:T(1,128)}, u32[]{:S(2)}, u32[]{:S(2)}) %all-to-all-start.11) | async-done | bytes 524320 | tf_op jit(solution)/shard_map/all_to_all | solution.py:121
  501.8 11.1 %all-to-all-done.12 = f32[32,1,4096]{2,1,0:T(1,128)} async-done(((f32[32,1,4096]{2,1,0:T(1,128)}), f32[32,1,4096]{2,1,0:T(1,128)}, u32[]{:S(2)}, u32[]{:S(2)}) %all-to-all-start.12) | async-done | bytes 524320 | tf_op jit(solution)/shard_map/all_to_all | solution.py:140
  546.6 7.4 subtract_bitcast_fusion
  570.9 11.8 %all-to-all-done.14 = f32[64,8,256]{2,0,1:T(8,128)S(1)} async-done(((f32[64,8,256]{2,0,1:T(8,128)}), f32[64,8,256]{2,0,1:T(8,128)S(1)}, u32[]{:S(2)}, u32[]{:S(2)}) %all-to-all-start.14) | async-done | bytes 524320 | tf_op jit(solution)/shard_map/all_to_all | solution.py:147
  586.4 15.0 %all-to-all-done.15 = f32[64,8,256]{2,0,1:T(8,128)S(1)} async-done(((f32[64,8,256]{2,0,1:T(8,128)}), f32[64,8,256]{2,0,1:T(8,128)S(1)}, u32[]{:S(2)}, u32[]{:S(2)}) %all-to-all-start.15) | async-done | bytes 524320 | tf_op jit(solution)/shard_map/all_to_all | solution.py:148
  605.1 13.3 %collective-permute-done = f32[2,2048,256]{2,1,0:T(8,128)} collective-permute-done((f32[2,2048,256]{2,1,0:T(8,128)}, f32[2,2048,256]{2,1,0:T(8,128)}, u32[]{:S(2)}, u32[]{:S(2)}) %collective-permute-start) | collective-permute-done | bytes 4194336 | tf_op jit(solution)/shard_map/ppermute | solution.py:26
  625.1 102.3 %collective-permute-done.1 = f32[2,2048,256]{2,1,0:T(8,128)} collective-permute-done((f32[2,2048,256]{2,1,0:T(8,128)}, f32[2,2048,256]{2,1,0:T(8,128)}, u32[]{:S(2)}, u32[]{:S(2)}) %collective-permute-start.1) | collective-permute-done | bytes 4194336 | tf_op jit(solution)/shard_map/ppermute | solution.py:28
  731.8 10.9 %fusion.549 = (f32[6,2048,2]{2,1,0:T(8,128)}, f32[6,2048,2]{2,1,0:T(8,128)}) fusion(f32[6,2048,256]{2,1,0:T(8,128)} %constant_dynamic-update-slice_fusion), kind=kLoop, calls=%fused_computation.598 | loop fusion | bytes 393216 | tf_op jit(solution)/shard_map/slice | solution.py:23
  781.1 24.6 %add_add_fusion = (f32[6,2048,260]{2,1,0:T(8,128)}, f32[6,2048,260]{2,1,0:T(8,128)}) fusion(f32[2048,260]{1,0:T(8,128)} %copy.547, f32[6]{0:T(128)S(1)} %get-tuple-element.51, f32[2048,260]{1,0:T(8,128)S(1)} %copy.546, f32[6]{0:T(128)S(1)} %get-tuple-element.52, f32[6,2048,2]{2,1,0:T(8,128)} %copy.438, f32[6,2048,256]{2,1,0:T(8,128)} %constant_dynamic-update-slice_fusion, ...), kind=kLoop, calls=%fused_computation.2 | loop fusion | flops 19169280 | bytes 42598448 | tf_op jit(solution)/shard_map/add | solution.py:169
  805.8 36.2 %fusion.8 = f32[4,2050,258]{2,1,0:T(8,128)} fusion(f32[6,2048,260]{2,1,0:T(8,128)} %get-tuple-element.15, f32[6,2048,260]{2,1,0:T(8,128)} %get-tuple-element.14, f32[258]{0:T(512)S(1)} %fusion.273, f32[2050]{0:T(1024)S(1)} %fusion.216, f32[4]{0:T(128)S(1)} %and_select_fusion.1), kind=kLoop, calls=%fused_computation.17 | loop fusion | flops 19040400 | bytes 34030688 | tf_op jit(solution)/shard_map/mul | solution.py:192
  842.0 19.0 %fusion.547 = (f32[2048,256]{1,0:T(8,128)S(1)}, f32[2,2048,256]{2,1,0:T(8,128)}) fusion(f32[256]{0:T(256)S(1)} %and_convert_fusion, f32[2048]{0:T(1024)S(1)} %fusion.269, f32[2]{0:T(128)S(1)} %and_select_fusion, f32[4,2050,258]{2,1,0:T(8,128)} %fusion.8, f32[6,2048,260]{2,1,0:T(8,128)} %get-tuple-element.14), kind=kLoop, calls=%fused_computation.597 | loop fusion | flops 9961472 | bytes 35660808 | tf_op jit(solution)/shard_map/reduce_sum | solution.py:194
  862.9 37.0 %reduce-scatter.2.cloned.1.call-done = f32[512,256]{0,1:T(8,128)} async-done(((f32[2048,256]{0,1:T(8,128)}), f32[512,256]{0,1:T(8,128)}) %reduce-scatter.2.cloned.1.call-update) | async-done | bytes 524304 | tf_op jit(solution)/shard_map/reduce_scatter | solution.py:195
  (241 shorter events, 437.5 us)
Async XLA Ops:
  28.9 19.5 %all-to-all-start = ((f32[8,64,256]{2,1,0:T(8,128)}), f32[8,64,256]{2,1,0:T(8,128)}, u32[]{:S(2)}, u32[]{:S(2)}) async-start(f32[8,64,256]{2,1,0:T(8,128)} %bitcast.450), calls=%async_computation | async-start | bytes 1048576 | tf_op jit(solution)/shard_map/all_to_all | solution.py:115
  82.5 19.8 %all-to-all-start.2 = ((f32[32,1,4096]{2,1,0:T(1,128)}), f32[32,1,4096]{2,1,0:T(1,128)S(1)}, u32[]{:S(2)}, u32[]{:S(2)}) async-start(f32[32,1,4096]{2,1,0:T(1,128)} %reshape.346), calls=%async_computation.2 | async-start | bytes 1048576 | tf_op jit(solution)/shard_map/all_to_all | solution.py:120
  102.2 18.8 %all-to-all-start.3 = ((f32[32,1,4096]{2,1,0:T(1,128)}), f32[32,1,4096]{2,1,0:T(1,128)S(1)}, u32[]{:S(2)}, u32[]{:S(2)}) async-start(f32[32,1,4096]{2,1,0:T(1,128)} %reshape.348), calls=%async_computation.3 | async-start | bytes 1048576 | tf_op jit(solution)/shard_map/all_to_all | solution.py:121
  192.9 18.8 %all-to-all-start.4 = ((f32[32,1,4096]{2,1,0:T(1,128)}), f32[32,1,4096]{2,1,0:T(1,128)S(1)}, u32[]{:S(2)}, u32[]{:S(2)}) async-start(f32[32,1,4096]{2,1,0:T(1,128)} %reshape.352), calls=%async_computation.4 | async-start | bytes 1048576 | tf_op jit(solution)/shard_map/all_to_all | solution.py:140
  211.8 18.8 %all-to-all-start.5 = ((f32[32,1,4096]{2,1,0:T(1,128)}), f32[32,1,4096]{2,1,0:T(1,128)S(1)}, u32[]{:S(2)}, u32[]{:S(2)}) async-start(f32[32,1,4096]{2,1,0:T(1,128)} %reshape.350), calls=%async_computation.5 | async-start | bytes 1048576 | tf_op jit(solution)/shard_map/all_to_all | solution.py:141
  260.7 18.8 %all-to-all-start.6 = ((f32[64,8,256]{2,0,1:T(8,128)}), f32[64,8,256]{2,0,1:T(8,128)S(1)}, u32[]{:S(2)}, u32[]{:S(2)}) async-start(f32[64,8,256]{2,0,1:T(8,128)} %copy.482), calls=%async_computation.6 | async-start | bytes 1048576 | tf_op jit(solution)/shard_map/all_to_all | solution.py:147
  279.5 18.8 %all-to-all-start.7 = ((f32[64,8,256]{2,0,1:T(8,128)}), f32[64,8,256]{2,0,1:T(8,128)S(1)}, u32[]{:S(2)}, u32[]{:S(2)}) async-start(f32[64,8,256]{2,0,1:T(8,128)} %copy.487), calls=%async_computation.7 | async-start | bytes 1048576 | tf_op jit(solution)/shard_map/all_to_all | solution.py:148
  300.5 18.8 %all-to-all-start.9 = ((f32[8,64,256]{2,1,0:T(8,128)}), f32[8,64,256]{2,1,0:T(8,128)S(1)}, u32[]{:S(2)}, u32[]{:S(2)}) async-start(f32[8,64,256]{2,1,0:T(8,128)} %bitcast.67), calls=%async_computation.9 | async-start | bytes 1048576 | tf_op jit(solution)/shard_map/all_to_all | solution.py:116
  319.2 19.0 %all-to-all-start.8 = ((f32[8,64,256]{2,1,0:T(8,128)}), f32[8,64,256]{2,1,0:T(8,128)S(1)}, u32[]{:S(2)}, u32[]{:S(2)}) async-start(f32[8,64,256]{2,1,0:T(8,128)} %bitcast.64), calls=%async_computation.8 | async-start | bytes 1048576 | tf_op jit(solution)/shard_map/all_to_all | solution.py:115
  367.9 18.8 %all-to-all-start.10 = ((f32[32,1,4096]{2,1,0:T(1,128)}), f32[32,1,4096]{2,1,0:T(1,128)S(1)}, u32[]{:S(2)}, u32[]{:S(2)}) async-start(f32[32,1,4096]{2,1,0:T(1,128)} %reshape.356), calls=%async_computation.10 | async-start | bytes 1048576 | tf_op jit(solution)/shard_map/all_to_all | solution.py:120
  386.7 19.7 %all-to-all-start.11 = ((f32[32,1,4096]{2,1,0:T(1,128)}), f32[32,1,4096]{2,1,0:T(1,128)}, u32[]{:S(2)}, u32[]{:S(2)}) async-start(f32[32,1,4096]{2,1,0:T(1,128)} %reshape.354), calls=%async_computation.11 | async-start | bytes 1048576 | tf_op jit(solution)/shard_map/all_to_all | solution.py:121
  493.4 19.6 %all-to-all-start.12 = ((f32[32,1,4096]{2,1,0:T(1,128)}), f32[32,1,4096]{2,1,0:T(1,128)}, u32[]{:S(2)}, u32[]{:S(2)}) async-start(f32[32,1,4096]{2,1,0:T(1,128)} %reshape.358), calls=%async_computation.12 | async-start | bytes 1048576 | tf_op jit(solution)/shard_map/all_to_all | solution.py:140
  513.0 18.9 %all-to-all-start.13 = ((f32[32,1,4096]{2,1,0:T(1,128)}), f32[32,1,4096]{2,1,0:T(1,128)S(1)}, u32[]{:S(2)}, u32[]{:S(2)}) async-start(f32[32,1,4096]{2,1,0:T(1,128)} %reshape.360), calls=%async_computation.13 | async-start | bytes 1048576 | tf_op jit(solution)/shard_map/all_to_all | solution.py:141
  515.6 240.4 %all-gather.3.cloned.1.call-start = ((), (), s32[]{:S(2)}) async-start(), calls=%async_computation.17 | async-start | bytes 2621440 | tf_op jit(solution)/shard_map/all_gather | solution.py:156
  515.6 102.7 %collective-permute-start = (f32[2,2048,256]{2,1,0:T(8,128)}, f32[2,2048,256]{2,1,0:T(8,128)}, u32[]{:S(2)}, u32[]{:S(2)}) collective-permute-start(f32[2,2048,256]{2,1,0:T(8,128)} %param.8), channel_id=1, source_target_pairs={{0,8},{8,16},{16,24},{1,9},{9,17},{17,25},{2,10},{10,18},{18,26},{... | collective-permute-start | bytes 12582920 | tf_op jit(solution)/shard_map/ppermute | solution.py:26
  521.2 206.2 %collective-permute-start.1 = (f32[2,2048,256]{2,1,0:T(8,128)}, f32[2,2048,256]{2,1,0:T(8,128)}, u32[]{:S(2)}, u32[]{:S(2)}) collective-permute-start(f32[2,2048,256]{2,1,0:T(8,128)} %param.8), channel_id=1, source_target_pairs={{8,0},{16,8},{24,16},{9,1},{17,9},{25,17},{10,2},{18,10},{26,18},{... | collective-permute-start | bytes 12582920 | tf_op jit(solution)/shard_map/ppermute | solution.py:28
  563.9 18.8 %all-to-all-start.14 = ((f32[64,8,256]{2,0,1:T(8,128)}), f32[64,8,256]{2,0,1:T(8,128)S(1)}, u32[]{:S(2)}, u32[]{:S(2)}) async-start(f32[64,8,256]{2,0,1:T(8,128)} %copy.537), calls=%async_computation.14 | async-start | bytes 1048576 | tf_op jit(solution)/shard_map/all_to_all | solution.py:147
  582.7 18.8 %all-to-all-start.15 = ((f32[64,8,256]{2,0,1:T(8,128)}), f32[64,8,256]{2,0,1:T(8,128)S(1)}, u32[]{:S(2)}, u32[]{:S(2)}) async-start(f32[64,8,256]{2,0,1:T(8,128)} %copy.542), calls=%async_computation.15 | async-start | bytes 1048576 | tf_op jit(solution)/shard_map/all_to_all | solution.py:148
  586.2 169.8 %all-gather.5.cloned.1.call-start = ((), (), s32[]{:S(2)}) async-start(), calls=%async_computation.18 | async-start | bytes 2621440 | tf_op jit(solution)/shard_map/all_gather | solution.py:156
  602.6 297.2 %reduce-scatter.2.cloned.1.call-start = ((), (), s32[]{:S(2)}) async-start(), calls=%async_computation.19 | async-start | bytes 2621440 | tf_op jit(solution)/shard_map/reduce_scatter | solution.py:195
  747.7 15.1 %collective-permute-start.2 = (f32[6,2048,2]{1,0,2:T(8,128)S(1)}, f32[6,2048,2]{1,0,2:T(8,128)S(1)}, u32[]{:S(2)}, u32[]{:S(2)}) collective-permute-start(f32[6,2048,2]{1,0,2:T(8,128)S(1)} %copy.435), channel_id=1, source_target_pairs={{0,1},{1,2},{2,3},{3,4},{4,5},{5,6},{6,7},{8,9},{9,10},{10,11},{11... | collective-permute-start | bytes 294920 | tf_op jit(solution)/shard_map/ppermute | solution.py:26
  754.6 12.2 %collective-permute-start.3 = (f32[6,2048,2]{1,0,2:T(8,128)S(1)}, f32[6,2048,2]{1,0,2:T(8,128)S(1)}, u32[]{:S(2)}, u32[]{:S(2)}) collective-permute-start(f32[6,2048,2]{1,0,2:T(8,128)S(1)} %copy.436), channel_id=1, source_target_pairs={{1,0},{2,1},{3,2},{4,3},{5,4},{6,5},{7,6},{9,8},{10,9},{11,10},{12... | collective-permute-start | bytes 294920 | tf_op jit(solution)/shard_map/ppermute | solution.py:28
  756.9 14.0 %collective-permute-start.4 = (f32[2,2048,2]{1,2,0:T(2,128)S(1)}, f32[2,2048,2]{1,2,0:T(2,128)S(1)}, u32[]{:S(2)}, u32[]{:S(2)}) collective-permute-start(f32[2,2048,2]{1,2,0:T(2,128)S(1)} %get-tuple-element.20), channel_id=1, source_target_pairs={{0,1},{1,2},{2,3},{3,4},{4,5},{5,6},{6,7},{8,9},{9,10},{10,11},{11... | collective-permute-start | bytes 98312 | tf_op jit(solution)/shard_map/ppermute | solution.py:26
  761.3 9.7 %collective-permute-start.5 = (f32[2,2048,2]{1,2,0:T(2,128)S(1)}, f32[2,2048,2]{1,2,0:T(2,128)S(1)}, u32[]{:S(2)}, u32[]{:S(2)}) collective-permute-start(f32[2,2048,2]{1,2,0:T(2,128)S(1)} %get-tuple-element.21), channel_id=1, source_target_pairs={{1,0},{2,1},{3,2},{4,3},{5,4},{6,5},{7,6},{9,8},{10,9},{11,10},{12... | collective-permute-start | bytes 98312 | tf_op jit(solution)/shard_map/ppermute | solution.py:28
  (8 other events, 519.8 us)
Sparse Core Ops, SparseCore 0:
  522.9 127.1 all-gather.2
  652.5 93.0 all-gather.4
  863.0 36.7 reduce-scatter.1
where the time goes:
time: 925 us; the launch traced here: 912 us
  waiting for transfers between devices  331 us (36%)
  matrix products  203 us (22%)
  local copies, waits for them, and re-layouts  156 us (17%)
  other arithmetic  120 us (13%)
  starting transfers between devices  64.9 us (7%)
  blocking collectives  21.7 us (2%)
  between operations  15 us (2%)
    dot_general x32, matrix products, section_one(): return jnp.einsum('...np,kn->...kp', values, table, precision=highest)  133 us
    ppermute x3, waiting for transfers between devices, padded(): lax.ppermute(head, axis, [((i + 1) % count, i) for i in range(ends)])  102 us
    dot_general x32, matrix products, section_two(): return jnp.einsum('...kp,jp->...kj', values, table, precision=highest)  70.6 us
    reduce_scatter x1, waiting for transfers between devices, shards(): lax.psum_scatter(running_total, 'row', scatter_dimension=0, tiled=True)  37 us
    mul x3, other arithmetic, shards(): present_warmth * zmask[:, None, None] * xmask[None, :, None]  36.2 us
    unnamed x38, local copies, waits for them, and re-layouts  32.3 us
    all_to_all x2, waiting for transfers between devices, shards(): lax.all_to_all(imag_part, 'col', split_axis=1, concat_axis=0, tiled=True)  28.8 us
    all_to_all x2, waiting for transfers between devices, shards(): lax.all_to_all(imag_part, ('row', 'col'), split_axis=1, concat_axis=0, ti...  25.7 us
  transfers between devices with their start and end apart: 24, of which 18 were waited for; matrix products, arithmetic and copies ran while one was open for 14% of the time, Pallas kernels for 0%

commit v1 on v0

v1 whole, which is shorter than its diff:
```python
import functools
import math

import jax
import jax.numpy as jnp
from jax import lax
from jax.experimental import pallas as pl
from jax.experimental.pallas import tpu as pltpu
from jax.sharding import PartitionSpec as P

STEPS = 2
FLUENCE_LIMIT = 2.0
GAIN_LENGTH = 0.2
INDEX_SLOPE_DNDT = 0.3
RADIX = 8
VMEM = pl.BlockSpec(memory_space=pltpu.VMEM)


def swap(z):
    half = z.shape[-1] // 2
    if z.shape[-1] % 128 == 0:
        return pltpu.roll(z, half, z.ndim - 1)
    return jnp.concatenate([z[:, half:], z[:, :half]], axis=1)


def cmul(z, cosine, signed_sine):
    return z * cosine + swap(z) * signed_sine


def sign_row(width, first):
    lane = lax.broadcasted_iota(jnp.int32, (1, width), 1)
    return jnp.where(lane < width // 2, first, -first).astype(jnp.float32)


def dft8(z):
    width = z[0].shape[-1]
    sgn = sign_row(width, 1.0)
    root = math.sqrt(0.5)

    def rot(v):
        return swap(v) * sgn

    def dft4(p, q, r, s):
        a, b = p + r, p - r
        c, d = q + s, rot(q - s)
        return a + c, b + d, a - c, b - d

    even = dft4(z[0], z[2], z[4], z[6])
    odd = dft4(z[1], z[3], z[5], z[7])
    turned = (
        odd[0],
        (odd[1] + rot(odd[1])) * root,
        rot(odd[2]),
        (rot(odd[3]) - odd[3]) * root,
    )
    return [even[i] + turned[i] for i in range(4)] + [even[i] - turned[i] for i in range(4)]


def split2(x):
    high = x.astype(jnp.bfloat16)
    low = (x - high.astype(jnp.float32)).astype(jnp.bfloat16)
    return high, low


def fresnel_body(gain, *refs):
    if gain:
        x, prec, pres, whi, wlo, twc, tws, postc, posts, g, out, heat, mid = refs
    else:
        x, prec, pres, whi, wlo, twc, tws, postc, posts, out, mid = refs
    size = x.shape[1]
    width = x.shape[2]
    neg = sign_row(width, -1.0)

    def column(n1, carry):
        v = cmul(x[n1], prec[n1], pres[n1])
        hi, lo = split2(v)
        dot = functools.partial(jnp.dot, preferred_element_type=jnp.float32)
        y = dot(whi[...], hi) + dot(whi[...], lo) + dot(wlo[...], hi)
        y = y[:size] + swap(y[size:]) * neg
        mid[n1] = cmul(y, twc[n1], tws[n1])
        return carry

    lax.fori_loop(0, RADIX, column, 0)
    step = 32

    def block(i, carry):
        at = pl.multiple_of(i * step, step)
        rows = pl.ds(at, step)
        y = dft8([mid[n, rows, :] for n in range(RADIX)])
        for k in range(RADIX):
            v = cmul(y[k], postc[k, rows, :], posts[k, rows, :])
            if gain:
                square = v * v
                irradiance = square + swap(square)
                bleach = g[k, rows, :] / (1.0 + irradiance / FLUENCE_LIMIT)
                heat[k, rows, :] = bleach * irradiance
                v = v * jnp.exp(0.5 * GAIN_LENGTH * bleach)
            out[k, rows, :] = v
        return carry

    lax.fori_loop(0, size // step, block, 0)


def fresnel(x, tables, gain=None):
    count, width = x.shape
    size = count // RADIX
    shape = jax.ShapeDtypeStruct((RADIX, size, width), jnp.float32)
    cells = x.reshape(size, RADIX, width).transpose(1, 0, 2)
    args = (cells,) + tables
    outs = [shape]
    if gain is not None:
        args = args + (gain.reshape(RADIX, size, width),)
        outs = [shape, shape]
    result = pl.pallas_call(
        functools.partial(fresnel_body, gain is not None),
        out_shape=outs,
        in_specs=[VMEM] * len(args),
        out_specs=[VMEM] * len(outs),
        scratch_shapes=[pltpu.VMEM((RADIX, size, width), jnp.float32)],
        cost_estimate=pl.CostEstimate(
            flops=6 * 2 * size * size * RADIX * width,
            bytes_accessed=32 * count * width,
            transcendentals=0,
        ),
    )(*args)
    result = [r.reshape(count, width) for r in result]
    return result[0] if gain is None else result


def make_tables(count, w):
    size = count // RADIX

    def wave(index, modulus, scale=1.0):
        angle = (index % modulus).astype(jnp.float32) * (2.0 * math.pi / modulus)
        return scale * jnp.cos(angle), scale * jnp.sin(angle)

    def packed(pair):
        cosine, sine = pair
        cosine, sine = cosine[..., None], sine[..., None]
        shape = cosine.shape[:-1] + (w,)
        cosine = jnp.broadcast_to(cosine, shape)
        sine = jnp.broadcast_to(sine, shape)
        return (
            jnp.concatenate([cosine, cosine], axis=-1),
            jnp.concatenate([-sine, sine], axis=-1),
        )

    outer = lax.iota(jnp.int32, RADIX)[:, None]
    inner = lax.iota(jnp.int32, size)[None, :]
    n = outer + RADIX * inner
    pre = packed(wave(n * n, 2 * count))
    twiddle = packed(wave(-outer * inner, count))
    k = outer * size + inner
    post = packed(wave(k * k - count // 4, 2 * count, 1.0 / math.sqrt(count)))
    square = lax.iota(jnp.int32, size)
    matrix = jnp.concatenate(wave(-square[:, None] * square[None, :], size), axis=0)
    coarse = lax.reduce_precision(matrix, 8, 7)
    high, low = coarse.astype(jnp.bfloat16), (matrix - coarse).astype(jnp.bfloat16)
    return pre + (high, low) + twiddle + post


def sweeps_body(cells, mask, out, first):
    planes = out.shape[0]
    rows, cols = out.shape[1], out.shape[2]
    height, width = cells.shape[1], cells.shape[2]

    def around(v):
        return (
            pltpu.roll(v, 1, 0)
            + pltpu.roll(v, height - 1, 0)
            + pltpu.roll(v, 1, 1)
            + pltpu.roll(v, width - 1, 1)
        )

    first[0] = jnp.zeros((height, width), jnp.float32)
    first[planes + 1] = jnp.zeros((height, width), jnp.float32)

    def one(z, carry):
        v = cells[z + 1]
        total = v + around(v) + cells[z] + cells[z + 2]
        first[z + 1] = total * mask[...]
        return carry

    lax.fori_loop(0, planes, one, 0)

    def two(z, carry):
        total = around(first[z + 1]) + first[z] + first[z + 2]
        out[z] = (cells[z + 1, :rows, :cols] + total[:rows, :cols]) / 7.0
        return carry

    lax.fori_loop(0, planes, two, 0)


def shift(x, axis, up):
    count = lax.axis_size(axis)
    if up:
        pairs = [(i, i + 1) for i in range(count - 1)]
    else:
        pairs = [(i + 1, i) for i in range(count - 1)]
    return lax.ppermute(x, axis, pairs)


def base_temperature(start):
    tile = lax.all_to_all(start, "row", split_axis=1, concat_axis=0, tiled=True)
    planes, rows, cols = tile.shape
    top = shift(tile[:, -8:], "row", True)
    bottom = shift(tile[:, :8], "row", False)
    tall = jnp.concatenate([tile, bottom, top], axis=1)
    right = shift(jnp.swapaxes(tall[:, :, :2], 1, 2), "col", False)
    left = shift(jnp.swapaxes(tall[:, :, -2:], 1, 2), "col", True)
    gap = jnp.zeros((planes, 124, rows + 16), jnp.float32)
    side = jnp.swapaxes(jnp.concatenate([right, gap, left], axis=1), 1, 2)
    cells = jnp.pad(jnp.concatenate([tall, side], axis=2), ((1, 1), (0, 0), (0, 0)))
    height, width = cells.shape[1:]
    row_index, col_index = lax.axis_index("row"), lax.axis_index("col")
    y = lax.iota(jnp.int32, height)
    x = lax.iota(jnp.int32, width)
    y = jnp.where(y < rows + 8, y, y - height) + row_index * rows
    x = jnp.where(x < cols + 64, x, x - width) + col_index * cols
    y_ok = (y >= 0) & (y < rows * lax.axis_size("row"))
    x_ok = (x >= 0) & (x < cols * lax.axis_size("col"))
    mask = jnp.where(y_ok[:, None] & x_ok[None, :], 1.0 / 7.0, 0.0).astype(jnp.float32)
    return pl.pallas_call(
        sweeps_body,
        out_shape=jax.ShapeDtypeStruct(tile.shape, jnp.float32),
        in_specs=[VMEM, VMEM],
        out_specs=VMEM,
        scratch_shapes=[pltpu.VMEM(cells.shape, jnp.float32)],
        cost_estimate=pl.CostEstimate(
            flops=20 * cells.size, bytes_accessed=12 * cells.size, transcendentals=0
        ),
    )(cells, mask)


def around_tile(heat):
    top = shift(heat[-1:], "row", True)
    bottom = shift(heat[:1], "row", False)
    left = shift(heat[:, -1].reshape(1, -1), "col", True).reshape(-1, 1)
    right = shift(heat[:, 0].reshape(1, -1), "col", False).reshape(-1, 1)
    return (
        jnp.concatenate([top, heat[:-1]], axis=0)
        + jnp.concatenate([heat[1:], bottom], axis=0)
        + jnp.concatenate([left, heat[:, :-1]], axis=1)
        + jnp.concatenate([heat[:, 1:], right], axis=1)
    )


def shards(cosine_part, sine_part, growth, start, pick):
    nr, nc = lax.axis_size("row"), lax.axis_size("col")
    nd = nr * nc
    rows, cols = cosine_part.shape
    count = rows * nr
    w = cols // nr
    both = ("row", "col")
    tables = make_tables(count, w)
    exchange = functools.partial(lax.all_to_all, split_axis=0, concat_axis=0)

    z = jnp.concatenate(
        [cosine_part.reshape(rows, nr, w), sine_part.reshape(rows, nr, w)], axis=2
    ).transpose(1, 0, 2)
    z = exchange(z, "row").reshape(count, 2 * w)
    gain = exchange(growth.reshape(nc, w, cols), "col")
    gain = gain.transpose(0, 2, 1).reshape(count, w)
    gain = jnp.concatenate([gain, gain], axis=1)

    z = fresnel(z, tables)
    z = exchange(z.reshape(nd, w, 2 * w), both)
    z = z.reshape(nr, nc, w, 2, w).transpose(1, 0, 4, 3, 2).reshape(count, 2 * w)
    z, heat_packed = fresnel(z, tables, gain)
    z = fresnel(z, tables)
    z = z.reshape(nc, nr, w, 2 * w).transpose(1, 0, 2, 3).reshape(nd, w, 2 * w)
    z = exchange(z, both)
    z = z.reshape(nd, w, 2, w).transpose(0, 3, 2, 1).reshape(count, 2 * w)
    heat0 = heat_packed[:, :w].reshape(nc, cols, w).transpose(0, 2, 1)
    heat0 = exchange(heat0, "col").reshape(rows, cols)
    base = base_temperature(start)
    z = fresnel(z, tables)
    z = exchange(z.reshape(nr, rows, 2 * w), "row").reshape(nr, rows, 2, w)
    real_part = z[:, :, 0].transpose(1, 0, 2).reshape(rows, cols)
    imag_part = z[:, :, 1].transpose(1, 0, 2).reshape(rows, cols)

    irradiance = real_part**2 + imag_part**2
    bleach = growth / (1.0 + irradiance / FLUENCE_LIMIT)
    heat1 = bleach * irradiance
    amplify = jnp.exp(0.5 * GAIN_LENGTH * bleach)
    real_part = real_part * amplify
    imag_part = imag_part * amplify

    planes = lax.iota(jnp.int32, base.shape[0])
    warm = base
    for step, heat in enumerate((heat0, heat1)):
        here = heat / 7.0 + around_tile(heat) / 49.0
        beside = heat / 49.0
        distance = jnp.abs(planes - pick[step])
        on = (distance == 0).astype(jnp.float32)[:, None, None]
        near = (distance == 1).astype(jnp.float32)[:, None, None]
        warm = warm + on * here[None] + near * beside[None]
    angle = INDEX_SLOPE_DNDT * jnp.sum(warm, axis=0)
    warm_out = lax.all_to_all(warm, "row", split_axis=0, concat_axis=1, tiled=True)
    c, s = jnp.cos(angle), jnp.sin(angle)
    return warm_out, real_part * c - imag_part * s, real_part * s + imag_part * c


def solution(mesh):
    placed = (P("row", "col"), P("row", "col"), P("row", "col"), P("row", None, "col"), P())
    return jax.shard_map(
        shards,
        mesh=mesh,
        in_specs=placed,
        out_specs=(P("row", None, "col"), P("row", "col"), P("row", "col")),
        check_vma=False,
    )
```

time: 925 us -> 352 us (0.38)
  waiting for transfers between devices: 331 us -> 108 us
  matrix products: 203 us -> 0 us
  local copies, waits for them, and re-layouts: 156 us -> 68.3 us
  other arithmetic: 120 us -> 36.8 us
  Pallas kernels: 0 us -> 60.8 us
  blocking collectives: 21.7 us -> 0 us
  between operations: 15 us -> 1.11 us
    dot_general x64 -> x0, matrix products: 203 us -> none  [the longest x32 133 us: section_one(): return jnp.einsum('...np,kn->...kp', values, table, precision=highest)]
    ppermute x6 -> x12, waiting for transfers between devices: 116 us -> 5.04 us  [shift(): return lax.ppermute(x, axis, pairs)]
    all_to_all x15 -> x8, waiting for transfers between devices: 178 us -> 103 us  [the longest x1 43.4 us: shards(): lax.all_to_all(warm, 'row', split_axis=0, concat_axis=1, tiled=True)]
    pallas_call x0 -> x5, Pallas kernels: none -> 60.8 us  [the longest x4 44.9 us: fresnel(): pl.pallas_call(functools.partial(fresnel_body, gain is not None), out_sha...]
    mul x6 -> x2, other arithmetic: 38.3 us -> 0.01 us  [the longest x1 0.01 us: make_tables(): n = outer + RADIX * inner]
    reduce_scatter x1 -> x0, waiting for transfers between devices: 37 us -> none  [shards(): lax.psum_scatter(running_total, 'row', scatter_dimension=0, tiled=True)]
    add x3, other arithmetic: 34.6 us -> 8.28 us  [the longest x1 4.32 us: shards(): real_part * s + imag_part * c]
    all_to_all x1 -> x0, blocking collectives: 21.7 us -> none  [shards(): lax.all_to_all(imag_part, 'col', split_axis=0, concat_axis=1, tiled=True)]
  transfers between devices with their start and end apart: 24 -> 20, of which waited for: 18 -> 6; matrix products, arithmetic and copies ran while one was open for 14% -> 24% of each run, Pallas kernels for 0% -> 18%
where the time goes in v1:
time: 352 us; the launch traced here: 347 us
  waiting for transfers between devices  108 us (31%)
  starting transfers between devices  71.3 us (20%)
  local copies, waits for them, and re-layouts  68.3 us (19%)
  Pallas kernels  60.8 us (17%)
  other arithmetic  36.8 us (10%)
    pallas_call x4, Pallas kernels, fresnel(): pl.pallas_call(functools.partial(fresnel_body, gain is not None), out_sha...  44.9 us
    all_to_all x1, waiting for transfers between devices, shards(): lax.all_to_all(warm, 'row', split_axis=0, concat_axis=1, tiled=True)  43.4 us
    ppermute x12, starting transfers between devices, shift(): return lax.ppermute(x, axis, pairs)  31.9 us
    all_to_all x1, waiting for transfers between devices, base_temperature(): tile = lax.all_to_all(start, 'row', split_axis=1, concat_axis=0, tiled=True)  22.6 us
    all_to_all x1, waiting for transfers between devices, shards(): z = exchange(z.reshape(nd, w, 2 * w), both)  18.7 us
    pallas_call x1, Pallas kernels, base_temperature(): pl.pallas_call(sweeps_body, out_shape=jax.ShapeDtypeStruct(tile.shape, jn...  15.9 us
    unnamed x13, local copies, waits for them, and re-layouts  14.5 us
    another operation x6, local copies, waits for them, and re-layouts, fresnel(): cells = x.reshape(size, RADIX, width).transpose(1, 0, 2)  11.1 us
  transfers between devices with their start and end apart: 20, of which 6 were waited for; matrix products, arithmetic and copies ran while one was open for 24% of the time, Pallas kernels for 18%

profile of v1, /device:TPU:0, one launch (start us, length us, event | category | flops | bytes accessed | tf_op | source)
XLA Modules:
  0.0 346.6 jit_solution(1748378202206887329)
XLA Ops:
  4.2 5.2 %all-to-all-start.1 = ((f32[4,512,128]{1,2,0:T(8,128)}), f32[4,512,128]{1,2,0:T(8,128)S(1)}, u32[]{:S(2)}, u32[]{:S(2)}) async-start(f32[4,512,128]{1,2,0:T(8,128)} %maximum_bitcast_fusion.1), calls=%async_computation.1 | async-start | bytes 2097152 | tf_op jit(solution)/shard_map/all_to_all | solution.py:261
  14.4 8.6 %all-to-all-done.1 = f32[4,512,128]{1,2,0:T(8,128)S(1)} async-done(((f32[4,512,128]{1,2,0:T(8,128)}), f32[4,512,128]{1,2,0:T(8,128)S(1)}, u32[]{:S(2)}, u32[]{:S(2)}) %all-to-all-start.1) | async-done | bytes 1048608 | tf_op jit(solution)/shard_map/all_to_all | solution.py:261
  23.0 4.9 %all-to-all-start.3 = ((f32[8,64,256]{2,1,0:T(8,128)}), f32[8,64,256]{2,1,0:T(8,128)S(1)}, u32[]{:S(2)}, u32[]{:S(2)}) async-start(f32[8,64,256]{2,1,0:T(8,128)} %bitcast.16), calls=%async_computation.3 | async-start | bytes 1048576 | tf_op jit(solution)/shard_map/all_to_all | solution.py:262
  35.6 10.9 %shard_map.77 = f32[8,256,128]{2,1,0:T(8,128)} custom-call(f32[8,256,128]{2,1,0:T(8,128)} %bitcast.85, f32[8,256,128]{2,1,0:T(8,128)} %get-tuple-element.55.refs_1_, f32[8,256,128]{2,1,0:T(8,128)} %get-tuple-element.56.refs_2_, bf16[512,256]{1,0:T(8,128)(2,1)} %get-tuple-element.41.refs_3_, bf16[512,256]{1,0:T(8,128)(2,1)} %get-tuple-element.40.refs_4_, ...), custom_call_target="tpu_custom_call" | custom-call | flops 805306368 | bytes 8388608 | tf_op jit(solution)/shard_map/pallas_call | solution.py:114
  47.3 5.1 %all-to-all-start.2 = ((f32[32,64,128]{2,1,0:T(8,128)}), f32[32,64,128]{2,1,0:T(8,128)S(1)}, u32[]{:S(2)}, u32[]{:S(2)}) async-start(f32[32,64,128]{2,1,0:T(8,128)} %bitcast.82), calls=%async_computation.2 | async-start | bytes 2097152 | tf_op jit(solution)/shard_map/all_to_all | solution.py:267
  52.4 8.7 %copy.84 = f32[2,2048,256]{2,0,1:T(2,128)} copy(f32[2,2048,256]{2,1,0:T(8,128)} %param.8) | data formatting | bytes 8388608 | tf_op args[3]
  61.1 18.7 %all-to-all-done.2 = f32[32,64,128]{2,1,0:T(8,128)S(1)} async-done(((f32[32,64,128]{2,1,0:T(8,128)}), f32[32,64,128]{2,1,0:T(8,128)S(1)}, u32[]{:S(2)}, u32[]{:S(2)}) %all-to-all-start.2) | async-done | bytes 1048608 | tf_op jit(solution)/shard_map/all_to_all | solution.py:267
  79.8 5.1 %all-to-all-start = ((f32[2,2048,256]{2,0,1:T(2,128)}), f32[2,2048,256]{2,0,1:T(2,128)}, u32[]{:S(2)}, u32[]{:S(2)}) async-start(f32[2,2048,256]{2,0,1:T(2,128)} %copy.84), calls=%async_computation | async-start | bytes 8388608 | tf_op jit(solution)/shard_map/all_to_all | solution.py:204
  95.1 12.3 %shard_map.78 = (f32[8,256,128]{2,1,0:T(8,128)}, f32[8,256,128]{2,1,0:T(8,128)}) custom-call(f32[8,256,128]{2,1,0:T(8,128)} %bitcast.86, f32[8,256,128]{2,1,0:T(8,128)} %get-tuple-element.55.refs_1_, f32[8,256,128]{2,1,0:T(8,128)} %get-tuple-element.56.refs_2_, bf16[512,256]{1,0:T(8,128)(2,1)} %get-tuple-element.41.refs_3_, ...), custom_call_target="tpu_custom_call" | custom-call | flops 805306368 | bytes 8388608 | tf_op jit(solution)/shard_map/pallas_call | solution.py:114
  109.7 22.6 %all-to-all-done = f32[2,2048,256]{2,0,1:T(2,128)} async-done(((f32[2,2048,256]{2,0,1:T(2,128)}), f32[2,2048,256]{2,0,1:T(2,128)}, u32[]{:S(2)}, u32[]{:S(2)}) %all-to-all-start) | async-done | bytes 4194336 | tf_op jit(solution)/shard_map/all_to_all | solution.py:204
  146.5 4.5 %collective-permute-start.1 = (f32[8,8,256]{2,1,0:T(8,128)S(1)}, f32[8,8,256]{2,1,0:T(8,128)S(1)}, u32[]{:S(2)}, u32[]{:S(2)}) collective-permute-start(f32[8,8,256]{2,1,0:T(8,128)S(1)} %get-tuple-element.21), channel_id=1, source_target_pairs={{0,8},{8,16},{16,24},{1,9},{9,17},{17,25},{2,10},{10,18},{18,26},{... | collective-permute-start | bytes 196616 | tf_op jit(solution)/shard_map/ppermute | solution.py:200
  151.0 10.9 %shard_map.79 = f32[8,256,128]{2,1,0:T(8,128)} custom-call(f32[8,256,128]{2,1,0:T(8,128)} %bitcast.81, f32[8,256,128]{2,1,0:T(8,128)} %get-tuple-element.55.refs_1_, f32[8,256,128]{2,1,0:T(8,128)} %get-tuple-element.56.refs_2_, bf16[512,256]{1,0:T(8,128)(2,1)} %get-tuple-element.41.refs_3_, bf16[512,256]{1,0:T(8,128)(2,1)} %get-tuple-element.40.refs_4_, ...), custom_call_target="tpu_custom_call" | custom-call | flops 805306368 | bytes 8388608 | tf_op jit(solution)/shard_map/pallas_call | solution.py:114
  164.2 6.0 %all-to-all-start.5 = ((f32[32,64,128]{2,1,0:T(8,128)}), f32[32,64,128]{2,1,0:T(8,128)}, u32[]{:S(2)}, u32[]{:S(2)}) async-start(f32[32,64,128]{2,1,0:T(8,128)} %bitcast.28), calls=%async_computation.5 | async-start | bytes 2097152 | tf_op jit(solution)/shard_map/all_to_all | solution.py:272
  192.3 15.9 %shard_map.76 = f32[8,512,256]{2,1,0:T(8,128)} custom-call(f32[10,528,384]{2,1,0:T(8,128)} %select_maximum_fusion.cells, f32[528,384]{1,0:T(8,128)} %and_select_fusion.mask), custom_call_target="tpu_custom_call" | custom-call | flops 40550400 | bytes 24330240 | tf_op jit(solution)/shard_map/pallas_call | solution.py:223
  209.8 7.1 %collective-permute-start.6 = (f32[1,512]{1,0:T(1,128)S(1)}, f32[1,512]{1,0:T(1,128)S(1)}, u32[]{:S(2)}, u32[]{:S(2)}) collective-permute-start(f32[1,512]{1,0:T(1,128)S(1)} %bitcast.98), channel_id=1, source_target_pairs={{0,1},{1,2},{2,3},{3,4},{4,5},{5,6},{6,7},{8,9},{9,10},{10,11},{11... | collective-permute-start | bytes 6152 | tf_op jit(solution)/shard_map/ppermute | solution.py:200
  231.7 10.9 %shard_map.80 = f32[8,256,128]{2,1,0:T(8,128)} custom-call(f32[8,256,128]{2,1,0:T(8,128)} %bitcast.83, f32[8,256,128]{2,1,0:T(8,128)} %get-tuple-element.55.refs_1_, f32[8,256,128]{2,1,0:T(8,128)} %get-tuple-element.56.refs_2_, bf16[512,256]{1,0:T(8,128)(2,1)} %get-tuple-element.41.refs_3_, bf16[512,256]{1,0:T(8,128)(2,1)} %get-tuple-element.40.refs_4_, ...), custom_call_target="tpu_custom_call" | custom-call | flops 805306368 | bytes 8388608 | tf_op jit(solution)/shard_map/pallas_call | solution.py:114
  245.1 4.8 %all-to-all-start.6 = ((f32[4,512,128]{1,2,0:T(8,128)}), f32[4,512,128]{1,2,0:T(8,128)S(1)}, u32[]{:S(2)}, u32[]{:S(2)}) async-start(f32[4,512,128]{1,2,0:T(8,128)} %copy.105), calls=%async_computation.6 | async-start | bytes 2097152 | tf_op jit(solution)/shard_map/all_to_all | solution.py:278
  254.4 10.0 %all-to-all-done.6 = f32[4,512,128]{1,2,0:T(8,128)S(1)} async-done(((f32[4,512,128]{1,2,0:T(8,128)}), f32[4,512,128]{1,2,0:T(8,128)S(1)}, u32[]{:S(2)}, u32[]{:S(2)}) %all-to-all-start.6) | async-done | bytes 1048608 | tf_op jit(solution)/shard_map/all_to_all | solution.py:278
  276.2 5.0 %collective-permute-done.11 = f32[1,512]{1,0:T(1,128)S(1)} collective-permute-done((f32[1,512]{1,0:T(1,128)S(1)}, f32[1,512]{1,0:T(1,128)S(1)}, u32[]{:S(2)}, u32[]{:S(2)}) %collective-permute-start.11) | collective-permute-done | bytes 2080 | tf_op jit(solution)/shard_map/ppermute | solution.py:200
  283.7 5.8 %fusion.48 = (f32[512,256]{1,0:T(8,128)S(1)}, f32[8,512,256]{2,1,0:T(8,128)}) fusion(f32[512,256]{1,0:T(8,128)S(1)} %get-tuple-element.16, f32[8]{0:T(128)S(1)} %get-tuple-element.61, f32[512,256]{1,0:T(8,128)S(1)} %fusion.9, f32[8]{0:T(128)S(1)} %get-tuple-element.62, f32[512,256]{1,0:T(8,128)} %get-tuple-element.27, f32[8]{0:T(128)S(1)} %get-tuple-element.63, ...), kind=kLoop, calls=%fused_computation.115 | loop fusion | flops 9306112 | bytes 11010176 | tf_op jit(solution)/shard_map/reduce_sum | solution.py:298
  289.5 4.9 %all-to-all-start.7 = ((f32[8,512,256]{2,1,0:T(8,128)}), f32[8,512,256]{2,1,0:T(8,128)}, u32[]{:S(2)}, u32[]{:S(2)}) async-start(f32[8,512,256]{2,1,0:T(8,128)} %get-tuple-element.15), calls=%async_computation.7 | async-start | bytes 8388608 | tf_op jit(solution)/shard_map/all_to_all | solution.py:299
  294.3 4.3 %multiply_add_fusion.1 = (f32[512,256]{1,0:T(8,128)}, f32[512,256]{1,0:T(8,128)}) fusion(f32[512,256]{1,0:T(8,128)S(1)} %get-tuple-element.14, f32[512,256]{1,0:T(8,128)S(1)} %copy.106, f32[512,256]{1,0:T(8,128)S(1)} %copy.108, f32[512,256]{1,0:T(8,128)} %param.7), kind=kLoop, calls=%fused_computation.38 | loop fusion | flops 2097152 | bytes 3145728 | tf_op jit(solution)/shard_map/add | solution.py:301
  298.7 43.4 %all-to-all-done.7 = f32[8,512,256]{2,1,0:T(8,128)} async-done(((f32[8,512,256]{2,1,0:T(8,128)}), f32[8,512,256]{2,1,0:T(8,128)}, u32[]{:S(2)}, u32[]{:S(2)}) %all-to-all-start.7) | async-done | bytes 4194336 | tf_op jit(solution)/shard_map/all_to_all | solution.py:299
  342.1 4.5 %copy.112 = f32[2,4,512,256]{3,2,1,0:T(8,128)} copy(f32[2,4,512,256]{3,2,0,1:T(8,128)} %bitcast.42) | data formatting | bytes 8388608 | tf_op jit(solution)/shard_map/all_to_all | solution.py:299
  (111 shorter events, 105.4 us)
Async XLA Ops:
  4.2 18.8 %all-to-all-start.1 = ((f32[4,512,128]{1,2,0:T(8,128)}), f32[4,512,128]{1,2,0:T(8,128)S(1)}, u32[]{:S(2)}, u32[]{:S(2)}) async-start(f32[4,512,128]{1,2,0:T(8,128)} %maximum_bitcast_fusion.1), calls=%async_computation.1 | async-start | bytes 2097152 | tf_op jit(solution)/shard_map/all_to_all | solution.py:261
  23.0 23.5 %all-to-all-start.3 = ((f32[8,64,256]{2,1,0:T(8,128)}), f32[8,64,256]{2,1,0:T(8,128)S(1)}, u32[]{:S(2)}, u32[]{:S(2)}) async-start(f32[8,64,256]{2,1,0:T(8,128)} %bitcast.16), calls=%async_computation.3 | async-start | bytes 1048576 | tf_op jit(solution)/shard_map/all_to_all | solution.py:262
  47.3 32.6 %all-to-all-start.2 = ((f32[32,64,128]{2,1,0:T(8,128)}), f32[32,64,128]{2,1,0:T(8,128)S(1)}, u32[]{:S(2)}, u32[]{:S(2)}) async-start(f32[32,64,128]{2,1,0:T(8,128)} %bitcast.82), calls=%async_computation.2 | async-start | bytes 2097152 | tf_op jit(solution)/shard_map/all_to_all | solution.py:267
  61.1 23.8 %copy-start.3 = (f32[8,64,256]{2,1,0:T(8,128)S(1)}, f32[8,64,256]{2,1,0:T(8,128)}, u32[]{:S(2)}) copy-start(f32[8,64,256]{2,1,0:T(8,128)} %copy-done.2) | copy-start | bytes 1572868
  79.8 52.5 %all-to-all-start = ((f32[2,2048,256]{2,0,1:T(2,128)}), f32[2,2048,256]{2,0,1:T(2,128)}, u32[]{:S(2)}, u32[]{:S(2)}) async-start(f32[2,2048,256]{2,0,1:T(2,128)} %copy.84), calls=%async_computation | async-start | bytes 8388608 | tf_op jit(solution)/shard_map/all_to_all | solution.py:204
  95.1 40.8 %copy-start.4 = (s32[2]{0:T(128)S(1)}, s32[2]{0:T(128)}, u32[]{:S(2)}) copy-start(s32[2]{0:T(128)} %param.9) | copy-start | bytes 28
  132.3 31.9 %all-to-all-start.4 = ((f32[8,64,256]{2,1,0:T(8,128)}), f32[8,64,256]{2,1,0:T(8,128)S(1)}, u32[]{:S(2)}, u32[]{:S(2)}) async-start(f32[8,64,256]{2,1,0:T(8,128)} %copy.98), calls=%async_computation.4 | async-start | bytes 1048576 | tf_op jit(solution)/shard_map/all_to_all | solution.py:275
  143.1 2.0 copy-start
  145.2 25.1 %collective-permute-start = (f32[8,8,256]{2,1,0:T(8,128)S(1)}, f32[8,8,256]{2,1,0:T(8,128)S(1)}, u32[]{:S(2)}, u32[]{:S(2)}) collective-permute-start(f32[8,8,256]{2,1,0:T(8,128)S(1)} %get-tuple-element.20), channel_id=1, source_target_pairs={{8,0},{16,8},{24,16},{9,1},{17,9},{25,17},{10,2},{18,10},{26,18},{... | collective-permute-start | bytes 196616 | tf_op jit(solution)/shard_map/ppermute | solution.py:200
  146.5 23.8 %collective-permute-start.1 = (f32[8,8,256]{2,1,0:T(8,128)S(1)}, f32[8,8,256]{2,1,0:T(8,128)S(1)}, u32[]{:S(2)}, u32[]{:S(2)}) collective-permute-start(f32[8,8,256]{2,1,0:T(8,128)S(1)} %get-tuple-element.21), channel_id=1, source_target_pairs={{0,8},{8,16},{16,24},{1,9},{9,17},{17,25},{2,10},{10,18},{18,26},{... | collective-permute-start | bytes 196616 | tf_op jit(solution)/shard_map/ppermute | solution.py:200
  164.2 57.6 %all-to-all-start.5 = ((f32[32,64,128]{2,1,0:T(8,128)}), f32[32,64,128]{2,1,0:T(8,128)}, u32[]{:S(2)}, u32[]{:S(2)}) async-start(f32[32,64,128]{2,1,0:T(8,128)} %bitcast.28), calls=%async_computation.5 | async-start | bytes 2097152 | tf_op jit(solution)/shard_map/all_to_all | solution.py:272
  177.3 5.8 %collective-permute-start.2 = (f32[8,2,528]{2,0,1:T(8,128)S(1)}, f32[8,2,528]{2,0,1:T(8,128)S(1)}, u32[]{:S(2)}, u32[]{:S(2)}) collective-permute-start(f32[8,2,528]{2,0,1:T(8,128)S(1)} %copy.86), channel_id=1, source_target_pairs={{1,0},{2,1},{3,2},{4,3},{5,4},{6,5},{7,6},{9,8},{10,9},{11,10},{12... | collective-permute-start | bytes 101384 | tf_op jit(solution)/shard_map/ppermute | solution.py:200
  179.4 4.4 %collective-permute-start.3 = (f32[8,2,528]{2,0,1:T(8,128)S(1)}, f32[8,2,528]{2,0,1:T(8,128)S(1)}, u32[]{:S(2)}, u32[]{:S(2)}) collective-permute-start(f32[8,2,528]{2,0,1:T(8,128)S(1)} %copy.87), channel_id=1, source_target_pairs={{0,1},{1,2},{2,3},{3,4},{4,5},{5,6},{6,7},{8,9},{9,10},{10,11},{11... | collective-permute-start | bytes 101384 | tf_op jit(solution)/shard_map/ppermute | solution.py:200
  185.8 2.8 copy-start.1
  208.5 42.5 %collective-permute-start.7 = (f32[1,512]{1,0:T(1,128)S(1)}, f32[1,512]{1,0:T(1,128)S(1)}, u32[]{:S(2)}, u32[]{:S(2)}) collective-permute-start(f32[1,512]{1,0:T(1,128)S(1)} %bitcast.100), channel_id=1, source_target_pairs={{1,0},{2,1},{3,2},{4,3},{5,4},{6,5},{7,6},{9,8},{10,9},{11,10},{12... | collective-permute-start | bytes 6152 | tf_op jit(solution)/shard_map/ppermute | solution.py:200
  209.8 41.3 %collective-permute-start.6 = (f32[1,512]{1,0:T(1,128)S(1)}, f32[1,512]{1,0:T(1,128)S(1)}, u32[]{:S(2)}, u32[]{:S(2)}) collective-permute-start(f32[1,512]{1,0:T(1,128)S(1)} %bitcast.98), channel_id=1, source_target_pairs={{0,1},{1,2},{2,3},{3,4},{4,5},{5,6},{6,7},{8,9},{9,10},{10,11},{11... | collective-permute-start | bytes 6152 | tf_op jit(solution)/shard_map/ppermute | solution.py:200
  216.9 35.1 %collective-permute-start.4 = (f32[1,256]{1,0:T(1,128)S(1)}, f32[1,256]{1,0:T(1,128)S(1)}, u32[]{:S(2)}, u32[]{:S(2)}) collective-permute-start(f32[1,256]{1,0:T(1,128)S(1)} %get-tuple-element.33), channel_id=1, source_target_pairs={{0,8},{8,16},{16,24},{1,9},{9,17},{17,25},{2,10},{10,18},{18,26},{... | collective-permute-start | bytes 3080 | tf_op jit(solution)/shard_map/ppermute | solution.py:200
  220.3 31.7 %collective-permute-start.5 = (f32[1,256]{1,0:T(1,128)S(1)}, f32[1,256]{1,0:T(1,128)S(1)}, u32[]{:S(2)}, u32[]{:S(2)}) collective-permute-start(f32[1,256]{1,0:T(1,128)S(1)} %get-tuple-element.32), channel_id=1, source_target_pairs={{8,0},{16,8},{24,16},{9,1},{17,9},{25,17},{10,2},{18,10},{26,18},{... | collective-permute-start | bytes 3080 | tf_op jit(solution)/shard_map/ppermute | solution.py:200
  245.1 19.2 %all-to-all-start.6 = ((f32[4,512,128]{1,2,0:T(8,128)}), f32[4,512,128]{1,2,0:T(8,128)S(1)}, u32[]{:S(2)}, u32[]{:S(2)}) async-start(f32[4,512,128]{1,2,0:T(8,128)} %copy.105), calls=%async_computation.6 | async-start | bytes 2097152 | tf_op jit(solution)/shard_map/all_to_all | solution.py:278
  266.5 9.5 %collective-permute-start.10 = (f32[1,512]{1,0:T(1,128)S(1)}, f32[1,512]{1,0:T(1,128)S(1)}, u32[]{:S(2)}, u32[]{:S(2)}) collective-permute-start(f32[1,512]{1,0:T(1,128)S(1)} %bitcast.103), channel_id=1, source_target_pairs={{0,1},{1,2},{2,3},{3,4},{4,5},{5,6},{6,7},{8,9},{9,10},{10,11},{11... | collective-permute-start | bytes 6152 | tf_op jit(solution)/shard_map/ppermute | solution.py:200
  269.1 12.2 %collective-permute-start.11 = (f32[1,512]{1,0:T(1,128)S(1)}, f32[1,512]{1,0:T(1,128)S(1)}, u32[]{:S(2)}, u32[]{:S(2)}) collective-permute-start(f32[1,512]{1,0:T(1,128)S(1)} %bitcast.102), channel_id=1, source_target_pairs={{1,0},{2,1},{3,2},{4,3},{5,4},{6,5},{7,6},{9,8},{10,9},{11,10},{12... | collective-permute-start | bytes 6152 | tf_op jit(solution)/shard_map/ppermute | solution.py:200
  270.4 11.7 %collective-permute-start.8 = (f32[1,256]{1,0:T(1,128)S(1)}, f32[1,256]{1,0:T(1,128)S(1)}, u32[]{:S(2)}, u32[]{:S(2)}) collective-permute-start(f32[1,256]{1,0:T(1,128)S(1)} %get-tuple-element.39), channel_id=1, source_target_pairs={{0,8},{8,16},{16,24},{1,9},{9,17},{17,25},{2,10},{10,18},{18,26},{... | collective-permute-start | bytes 3080 | tf_op jit(solution)/shard_map/ppermute | solution.py:200
  273.7 8.4 %collective-permute-start.9 = (f32[1,256]{1,0:T(1,128)S(1)}, f32[1,256]{1,0:T(1,128)S(1)}, u32[]{:S(2)}, u32[]{:S(2)}) collective-permute-start(f32[1,256]{1,0:T(1,128)S(1)} %get-tuple-element.38), channel_id=1, source_target_pairs={{8,0},{16,8},{24,16},{9,1},{17,9},{25,17},{10,2},{18,10},{26,18},{... | collective-permute-start | bytes 3080 | tf_op jit(solution)/shard_map/ppermute | solution.py:200
  289.5 52.6 %all-to-all-start.7 = ((f32[8,512,256]{2,1,0:T(8,128)}), f32[8,512,256]{2,1,0:T(8,128)}, u32[]{:S(2)}, u32[]{:S(2)}) async-start(f32[8,512,256]{2,1,0:T(8,128)} %get-tuple-element.15), calls=%async_computation.7 | async-start | bytes 8388608 | tf_op jit(solution)/shard_map/all_to_all | solution.py:299
  (1 other events, 0.8 us)
